TPU v7x, 32 devices: a whole 2x2x4 slice. The times are simulated.
32 devices in a mesh: dp: 4 (over x, core), expert: 8 (over z, y).
Axes of the slice: x: 2, y: 2, z: 4, core: 2. Of those that a mesh axis runs over, the one named last changes fastest.
Arguments:
- dense_weights: bfloat16 [3, 5632, 2048], P(None, 'dp', 'expert'), may hold values from -0.125 to 0.125
- tokens: bfloat16 [1024, 2048], P('expert'), may hold values from -6 to 6
- cotangent: bfloat16 [1024, 2048], P('expert'), may hold values from -6 to 6
- routes: int32 [1024, 4], P('expert'), may hold values from 0 to 7, all different within a row; in each aligned block of 128 rows (0 to 127, 128 to 255, ...) at most 80 rows name the same one
- route_gates: float32 [1024, 4], P('expert'), may hold values from 0.2 to 1
- unit_perm: int32 [2, 5632], replicated, may hold values from 0 to 5631, as said below
- slab_owner: int32 [8], replicated, may hold values from 0 to 7, each once
Outputs:
- mixed: bfloat16 [1024, 2048], P('expert', 'dp')
- token_grad: bfloat16 [1024, 2048], P('expert', 'dp')
- expert_grad: bfloat16 [8, 3, 1408, 2048], P('expert', None, 'dp')
Inputs may be any that keep to these rules, and one draw needn't show every extreme that they name: `unit_perm`: each row is a permutation of the 5632 units. In every row, for every slab s and share g, the 352 positions s * 1408 + g * 352 up to s * 1408 + (g + 1) * 352 - 1 hold exactly 88 units of each block of 1408 consecutive units. `slab_owner`: each slab number c * 4 + s is owned by exactly one expert. `routes`: each row names 4 different experts. In each aligned block of 128 rows no expert is named more than 80 times, a bound that some block reaches.
All inputs are finite; a program needn't handle non-finite values.
Results may differ from a plain program's by a relative error of at most 0.013.
Values may be sent and summed in bfloat16 or wider, within the bound.
A program may use at most 128 MiB of HBM per device.

v0:
```python
import jax
import jax.numpy as jnp
from jax import lax
from jax.sharding import PartitionSpec as P

FF = 5632
EH = 1408


def silu_parts(preact):
    sigmoid_value = jax.nn.sigmoid(preact)
    return (preact * sigmoid_value, sigmoid_value * (1.0 + preact * (1.0 - sigmoid_value)))


def contract_last(left_side, right_side):
    return lax.dot_general(
        left_side, right_side, (((1,), (1,)), ((), ())), preferred_element_type=jnp.float32
    )


def contract_first(left_side, right_side):
    return lax.dot_general(
        left_side, right_side, (((0,), (0,)), ((), ())), preferred_element_type=jnp.float32
    )


def widen_rounded(values):
    return lax.optimization_barrier(values).astype(jnp.float32)


def body(dense_weights, tokens, cotangent, routes, route_gates, unit_perm, slab_owner):
    dp_count = lax.axis_size("dp")
    expert_count = lax.axis_size("expert")
    my_row = lax.axis_index("dp")
    my_col = lax.axis_index("expert")
    block_weights = lax.all_gather(dense_weights, "expert", axis=2, tiled=True)
    block_units = block_weights.shape[1]
    units_share = EH // dp_count
    pick_count = units_share // dp_count
    slab_count = FF // EH
    owned_slab = slab_owner[my_col]
    copy_id = owned_slab // slab_count
    slab_start = owned_slab % slab_count * EH
    shares = lax.dynamic_slice(unit_perm, (copy_id, slab_start), (1, EH)).reshape(
        dp_count, units_share
    )
    sort_order = jnp.argsort(shares // block_units, axis=1, stable=True)
    ordered = jnp.take_along_axis(shares, sort_order, axis=1).reshape(
        dp_count, dp_count, pick_count
    )
    my_units = lax.dynamic_index_in_dim(ordered, my_row, 1, keepdims=False) - my_row * block_units
    outgoing = jnp.take(block_weights, my_units.reshape(-1), axis=1)
    arrived = lax.all_to_all(outgoing, "dp", split_axis=1, concat_axis=1, tiled=True)
    my_order = lax.dynamic_index_in_dim(sort_order, my_row, 0, keepdims=False)
    expert_weights = jnp.take(arrived, jnp.argsort(my_order), axis=1)
    tok_rows = tokens.shape[0]
    route_count = routes.shape[1]
    copies = tok_rows * route_count
    capacity = copies * 5 // (4 * expert_count)
    flat_routes = routes.reshape(-1)
    onehot = (flat_routes[:, None] == jnp.arange(expert_count, dtype=jnp.int32)[None, :]).astype(
        jnp.int32
    )
    slot_rank = jnp.sum((jnp.cumsum(onehot, axis=0) - 1) * onehot, axis=1)
    slot_index = flat_routes * capacity + slot_rank
    source = (
        jnp.full((expert_count * capacity,), copies, jnp.int32)
        .at[slot_index]
        .set(jnp.arange(copies, dtype=jnp.int32))
    )
    filled = source < copies
    safe_rows = jnp.minimum(source, copies - 1)
    token_of = safe_rows // route_count
    pick_rows = jnp.where(filled, token_of, tok_rows)
    padded_tokens = jnp.concatenate([tokens, jnp.zeros((1, tokens.shape[1]), jnp.bfloat16)], axis=0)
    gate_of = jnp.where(filled, route_gates.reshape(-1)[safe_rows], jnp.zeros((), jnp.float32))
    send_x = padded_tokens[pick_rows]
    send_dy = (gate_of[:, None] * cotangent[token_of].astype(jnp.float32)).astype(jnp.bfloat16)
    recv_x, recv_dy = (
        lax.all_to_all(send_x, "expert", split_axis=0, concat_axis=0, tiled=True),
        lax.all_to_all(send_dy, "expert", split_axis=0, concat_axis=0, tiled=True),
    )
    w_gate = expert_weights[0]
    w_up = expert_weights[1]
    w_down = expert_weights[2]
    pre_gate = contract_last(recv_x, w_gate)
    pre_up = contract_last(recv_x, w_up)
    activation, silu_slope = silu_parts(pre_gate)
    hidden = (activation * pre_up).astype(jnp.bfloat16)
    out_part = jnp.dot(hidden, w_down, preferred_element_type=jnp.float32).astype(jnp.bfloat16)
    d_hidden = contract_last(recv_dy, w_down)
    d_gate = (d_hidden * pre_up * silu_slope).astype(jnp.bfloat16)
    d_up = (d_hidden * activation).astype(jnp.bfloat16)
    both_grads = jnp.concatenate([d_gate, d_up], axis=1)
    both_rows = jnp.concatenate([w_gate, w_up], axis=0)
    back_part = jnp.dot(both_grads, both_rows, preferred_element_type=jnp.float32).astype(
        jnp.bfloat16
    )
    weight_grads = jnp.stack(
        [
            contract_first(d_gate, recv_x),
            contract_first(d_up, recv_x),
            contract_first(hidden, recv_dy),
        ]
    ).astype(jnp.bfloat16)[None]
    shared_gate_w = block_weights[0]
    shared_up_w = block_weights[1]
    shared_down_w = block_weights[2]
    shared_gate = contract_last(tokens, shared_gate_w)
    shared_up = contract_last(tokens, shared_up_w)
    shared_act, shared_slope = silu_parts(shared_gate)
    shared_hidden = (shared_act * shared_up).astype(jnp.bfloat16)
    shared_out = jnp.dot(shared_hidden, shared_down_w, preferred_element_type=jnp.float32)
    shared_dh = contract_last(cotangent, shared_down_w)
    shared_dgate = (shared_dh * shared_up * shared_slope).astype(jnp.bfloat16)
    shared_dup = (shared_dh * shared_act).astype(jnp.bfloat16)
    shared_back = jnp.dot(
        shared_dgate, shared_gate_w, preferred_element_type=jnp.float32
    ) + jnp.dot(shared_dup, shared_up_w, preferred_element_type=jnp.float32)
    summed_out, summed_back = (
        lax.psum_scatter(
            widen_rounded(out_part).astype(jnp.bfloat16), "dp", scatter_dimension=1, tiled=True
        ).astype(jnp.float32),
        lax.psum_scatter(
            widen_rounded(back_part).astype(jnp.bfloat16), "dp", scatter_dimension=1, tiled=True
        ).astype(jnp.float32),
    )
    ret_out, ret_back = (
        lax.all_to_all(
            summed_out.astype(jnp.bfloat16), "expert", split_axis=0, concat_axis=0, tiled=True
        ).astype(summed_out.dtype),
        lax.all_to_all(
            summed_back.astype(jnp.bfloat16), "expert", split_axis=0, concat_axis=0, tiled=True
        ).astype(summed_back.dtype),
    )
    rows_out = ret_out[slot_index].reshape(tok_rows, route_count, -1)
    rows_back = ret_back[slot_index].reshape(tok_rows, route_count, -1)
    shared_slice, shared_grad = (
        lax.psum_scatter(
            shared_out.astype(jnp.bfloat16), "dp", scatter_dimension=1, tiled=True
        ).astype(jnp.float32),
        lax.psum_scatter(
            shared_back.astype(jnp.bfloat16), "dp", scatter_dimension=1, tiled=True
        ).astype(jnp.float32),
    )
    mixed = shared_slice + jnp.sum(route_gates[:, :, None] * rows_out, axis=1)
    token_grad = shared_grad + jnp.sum(rows_back, axis=1)
    return (mixed.astype(jnp.bfloat16), token_grad.astype(jnp.bfloat16), weight_grads)


def solution(mesh):
    in_specs = (
        P(None, "dp", "expert"),
        P("expert", None),
        P("expert", None),
        P("expert", None),
        P("expert", None),
        P(),
        P(),
    )
    out_specs = (P("expert", "dp"), P("expert", "dp"), P("expert", None, "dp", None))
    return jax.shard_map(body, mesh=mesh, in_specs=in_specs, out_specs=out_specs, check_vma=False)
```

profile of v0, /device:TPU:0, one launch (start us, length us, event | category | flops | bytes accessed | tf_op | source)
XLA Modules:
  0.0 804.3 jit_solution(1391486535818355225)
XLA Ops:
  7.2 12.2 %copy.24 = bf16[3,1408,256]{2,0,1:T(4,128)(2,1)} copy(bf16[3,1408,256]{2,1,0:T(8,128)(2,1)} %param.7) | data formatting | bytes 4325376 | tf_op args[0]
  21.8 2.4 scatter_custom_fusion
  24.3 4.3 gather_fusion.4
  28.7 4.1 gather_fusion
  32.9 7.8 all-to-all-start
  44.8 3.9 sort.34
  48.8 11.9 %gather_fusion.7 = s32[1408]{0:T(1024)S(1)} fusion(s32[4,352]{1,0:T(4,128)S(1)} %reshape.187, s32[1408]{0:T(1024)S(1)} %reshape.251), kind=kCustom, calls=%fused_computation.7 | custom fusion | bytes 22528 | tf_op jit(solution)/shard_map/jit(take_along_axis)/gather | solution.py:48
  62.3 430.4 %all-gather.2.cloned.1.call-done = bf16[3,1408,2048]{2,0,1:T(4,128)(2,1)} async-done(((bf16[3,1408,256]{2,0,1:T(4,128)(2,1)}), bf16[3,1408,2048]{2,0,1:T(4,128)(2,1)}) %all-gather.2.cloned.1.call-update) | async-done | bytes 17301520 | tf_op jit(solution)/shard_map/all_gather | solution.py:36
  492.7 21.0 %gather_fusion.1 = bf16[352,3,2048]{2,1,0:T(4,128)(2,1)} fusion(bf16[3,1408,2048]{2,0,1:T(4,128)(2,1)} %all-gather.2.cloned.1.call-done, s32[1024]{0:T(1024)S(1)} %pad_clamp_fusion.4), kind=kCustom, calls=%fused_computation.1 | custom fusion | bytes 8652160 | tf_op jit(solution)/shard_map/jit(_take)/gather | solution.py:52
  513.7 7.9 select_bitcast_fusion.1
  521.5 1.5 copy-done.3
  523.0 5.1 all-to-all-start.1
  528.3 3.4 gather_fusion.5
  531.7 2.0 fusion.12
  533.7 59.6 %all-to-all-done.1 = bf16[3,352,2048]{2,0,1:T(4,128)(2,1)} async-done(((bf16[3,352,2048]{2,0,1:T(4,128)(2,1)}), bf16[3,352,2048]{2,0,1:T(4,128)(2,1)}, u32[]{:S(2)}, u32[]{:S(2)}) %all-to-all-start.1) | async-done | bytes 4325408 | tf_op jit(solution)/shard_map/all_to_all | solution.py:53
  593.2 4.6 all-to-all-start.3
  598.4 3.8 sort.35
  602.2 16.0 %gather_fusion.2 = bf16[352,3,2048]{2,1,0:T(4,128)(2,1)} fusion(bf16[3,352,2048]{2,0,1:T(4,128)(2,1)} %all-to-all-done.1, s32[1024]{0:T(1024)S(1)} %pad_clamp_fusion.3), kind=kCustom, calls=%fused_computation.2 | custom fusion | bytes 8652160 | tf_op jit(solution)/shard_map/jit(_take)/gather | solution.py:55
  618.3 5.4 select_bitcast_fusion
  623.7 6.4 fusion.61
  630.9 2.0 copy.71
  633.7 2.3 fusion.62
  636.0 21.1 %all-to-all-done.3 = bf16[8,80,2048]{2,1,0:T(8,128)(2,1)} async-done(((bf16[8,80,2048]{2,1,0:T(8,128)(2,1)}), bf16[8,80,2048]{2,1,0:T(8,128)(2,1)}, u32[]{:S(2)}, u32[]{:S(2)}) %all-to-all-start.3) | async-done | bytes 2621472 | tf_op jit(solution)/shard_map/all_to_all | solution.py:81
  657.1 3.7 fusion.34
  660.9 2.5 multiply_convert_fusion.1
  664.2 3.2 convolution_convert_fusion.1
  667.5 5.8 convolution_convert_fusion
  673.4 43.0 %fusion.60 = (bf16[1,1408,2048]{2,0,1:T(2,128)(2,1)}, bf16[1,1408,2048]{2,0,1:T(2,128)(2,1)}, bf16[1,1408,2048]{2,0,1:T(2,128)(2,1)}) fusion(bf16[3,1408,2048]{2,0,1:T(4,128)(2,1)} %all-gather.2.cloned.1.call-done), kind=kLoop, calls=%fused_computation.121 | loop fusion | bytes 34603008 | tf_op jit(solution)/shard_map/slice | solution.py:106
  716.4 8.5 %fusion.10 = f32[128,1408]{1,0:T(8,128)S(1)} fusion(bf16[128,2048]{1,0:T(8,128)(2,1)S(1)} %copy-done.11, bf16[1,1408,2048]{2,0,1:T(2,128)(2,1)} %get-tuple-element.11), kind=kOutput, calls=%fused_computation.19 | convolution fusion | flops 738197504 | bytes 7012352 | tf_op jit(solution)/shard_map/dot_general | solution.py:16
  724.9 8.1 %fusion = f32[128,1408]{1,0:T(8,128)S(1)} fusion(bf16[128,2048]{1,0:T(8,128)(2,1)S(1)} %copy-done, bf16[1,1408,2048]{2,0,1:T(2,128)(2,1)} %get-tuple-element.12), kind=kOutput, calls=%fused_computation.9 | convolution fusion | flops 738197504 | bytes 7012352 | tf_op jit(solution)/shard_map/dot_general | solution.py:16
  733.0 3.7 fusion.6
  736.7 4.1 fusion.4
  740.9 4.6 fusion.22
  745.6 4.2 all-to-all-start.2
  749.8 8.9 %fusion.25 = bf16[128,2048]{1,0:T(8,128)(2,1)} fusion(bf16[1,1408,2048]{2,0,1:T(2,128)(2,1)} %get-tuple-element.12, f32[128,1408]{1,0:T(8,128)S(1)} %fusion.6, f32[128,1408]{1,0:T(8,128)S(1)} %fusion.10), kind=kOutput, calls=%fused_computation.39 | convolution fusion | flops 739540992 | bytes 7733248 | tf_op jit(solution)/shard_map/dot_general | solution.py:113
  758.8 4.4 fusion.18
  763.2 3.1 all-to-all-done.2
  766.4 4.4 all-to-all-start.4
  770.8 2.4 fusion.16
  773.2 1.3 fusion.17
  774.5 2.3 pad_maximum_fusion
  778.1 1.6 gather_fusion.3
  781.0 6.5 all-to-all-done.4
  788.8 1.6 gather_fusion.6
  790.5 1.3 reshape.191
  791.8 1.8 reduce_sum.32
  794.4 1.6 add_convert_fusion
  796.0 1.6 add_convert_fusion.1
  (108 shorter events, 13.6 us)
Async XLA Ops:
  7.2 521.1 %copy-start = (bf16[128,2048]{1,0:T(8,128)(2,1)S(1)}, bf16[128,2048]{1,0:T(8,128)(2,1)}, u32[]{:S(2)}) copy-start(bf16[128,2048]{1,0:T(8,128)(2,1)} %param.9) | copy-start | bytes 1572868
  7.2 12.3 %copy-start.12 = (s32[128,4]{0,1:T(4,128)S(1)}, s32[128,4]{0,1:T(4,128)}, u32[]{:S(2)}) copy-start(s32[128,4]{0,1:T(4,128)} %param.10) | copy-start | bytes 6148
  7.2 12.9 %copy-start.13 = (f32[128,4]{0,1:T(4,128)S(1)}, f32[128,4]{0,1:T(4,128)}, u32[]{:S(2)}) copy-start(f32[128,4]{0,1:T(4,128)} %param.11) | copy-start | bytes 6148
  7.2 485.5 %all-gather.2.cloned.1.call-start = ((), (), s32[]{:S(2)}) async-start(), calls=%async_computation.9 | async-start | bytes 25952256 | tf_op jit(solution)/shard_map/all_gather | solution.py:36
  19.5 9.1 %copy-start.10 = (bf16[128,2048]{1,0:T(8,128)(2,1)S(1)}, bf16[128,2048]{1,0:T(8,128)(2,1)}, u32[]{:S(2)}) copy-start(bf16[128,2048]{1,0:T(8,128)(2,1)} %param.8) | copy-start | bytes 1572868
  32.9 7.8 copy-start.14
  32.9 488.7 %all-to-all-start = ((bf16[8,80,2048]{2,1,0:T(8,128)(2,1)}), bf16[8,80,2048]{2,1,0:T(8,128)(2,1)S(1)}, u32[]{:S(2)}, u32[]{:S(2)}) async-start(bf16[8,80,2048]{2,1,0:T(8,128)(2,1)} %bitcast.87), calls=%async_computation.1 | async-start | bytes 5242880 | tf_op jit(solution)/shard_map/all_to_all | solution.py:80
  521.5 1.5 copy-start.3
  523.0 70.2 %all-to-all-start.1 = ((bf16[3,352,2048]{2,0,1:T(4,128)(2,1)}), bf16[3,352,2048]{2,0,1:T(4,128)(2,1)}, u32[]{:S(2)}, u32[]{:S(2)}) async-start(bf16[3,352,2048]{2,0,1:T(4,128)(2,1)} %select_bitcast_fusion.1), calls=%async_computation.2 | async-start | bytes 11534336 | tf_op jit(solution)/shard_map/all_to_all | solution.py:53
  593.2 63.9 %all-to-all-start.3 = ((bf16[8,80,2048]{2,1,0:T(8,128)(2,1)}), bf16[8,80,2048]{2,1,0:T(8,128)(2,1)}, u32[]{:S(2)}, u32[]{:S(2)}) async-start(bf16[8,80,2048]{2,1,0:T(8,128)(2,1)} %fusion.12), calls=%async_computation.6 | async-start | bytes 5242880 | tf_op jit(solution)/shard_map/all_to_all | solution.py:81
  597.8 147.8 %reduce-scatter.7.cloned.1.call-start = ((), (), s32[]{:S(2)}) async-start(), calls=%async_computation.11 | async-start | bytes 3276800 | tf_op jit(solution)/shard_map/reduce_scatter | solution.py:121
  630.9 2.0 copy-start.7
  630.9 2.8 copy-start.4
  657.1 3.7 copy-start.5
  657.1 3.7 copy-start.8
  657.1 3.7 copy-start.17
  663.4 0.8 copy-start.15
  667.5 95.8 %reduce-scatter.11.cloned.1.call-start = ((), (), s32[]{:S(2)}) async-start(), calls=%async_computation.13 | async-start | bytes 3276800 | tf_op jit(solution)/shard_map/reduce_scatter | solution.py:124
  673.4 43.0 %copy-start.11 = (bf16[128,2048]{1,0:T(8,128)(2,1)S(1)}, bf16[128,2048]{1,0:T(8,128)(2,1)}, u32[]{:S(2)}) copy-start(bf16[128,2048]{1,0:T(8,128)(2,1)} %param.8) | copy-start | bytes 1572868
  673.4 121.0 %reduce-scatter.9.cloned.1.call-start = ((), (), s32[]{:S(2)}) async-start(), calls=%async_computation.12 | async-start | bytes 655360 | tf_op jit(solution)/shard_map/reduce_scatter | solution.py:142
  716.4 16.6 %copy-start.1 = (bf16[1,1408,2048]{2,0,1:T(2,128)(2,1)S(1)}, bf16[1,1408,2048]{2,0,1:T(2,128)(2,1)}, u32[]{:S(2)}) copy-start(bf16[1,1408,2048]{2,0,1:T(2,128)(2,1)} %get-tuple-element.13) | copy-start | bytes 17301508
  724.9 16.0 %slice-start = ((s8[11534336]{0:T(1024)(128)(4,1)}), s8[3145728]{0:T(1024)(128)(4,1)S(1)}, s32[]{:S(2)}) async-start(s8[11534336]{0:T(1024)(128)(4,1)} %bitcast.85), calls=%async_computation.14 | async-start | bytes 6291456
  733.0 7.8 slice-start.1
  736.7 4.1 slice-start.2
  745.6 20.8 %all-to-all-start.2 = ((bf16[8,80,512]{2,1,0:T(8,128)(2,1)}), bf16[8,80,512]{2,1,0:T(8,128)(2,1)}, u32[]{:S(2)}, u32[]{:S(2)}) async-start(bf16[8,80,512]{2,1,0:T(8,128)(2,1)} %bitcast.98), calls=%async_computation.4 | async-start | bytes 1310720 | tf_op jit(solution)/shard_map/all_to_all | solution.py:129
  749.8 46.2 %reduce-scatter.5.cloned.1.call-start = ((), (), s32[]{:S(2)}) async-start(), calls=%async_computation.10 | async-start | bytes 655360 | tf_op jit(solution)/shard_map/reduce_scatter | solution.py:139
  758.8 12.0 %copy-start.6 = (bf16[8,80,2048]{2,1,0:T(8,128)(2,1)S(1)}, bf16[8,80,2048]{2,1,0:T(8,128)(2,1)}, u32[]{:S(2)}) copy-start(bf16[8,80,2048]{2,1,0:T(8,128)(2,1)} %copy-done.3) | copy-start | bytes 7864324
  766.4 21.2 %all-to-all-start.4 = ((bf16[8,80,512]{2,1,0:T(8,128)(2,1)}), bf16[8,80,512]{2,1,0:T(8,128)(2,1)}, u32[]{:S(2)}, u32[]{:S(2)}) async-start(bf16[8,80,512]{2,1,0:T(8,128)(2,1)} %bitcast.97), calls=%async_computation.8 | async-start | bytes 1310720 | tf_op jit(solution)/shard_map/all_to_all | solution.py:132
  770.8 2.4 copy-start.16
  773.1 1.4 copy-start.9
  790.4 3.2 copy-start.2
Sparse Core Ops, SparseCore 0:
  19.6 473.0 all-gather.1
  667.6 32.6 reduce-scatter.6
  702.8 34.3 reduce-scatter.10
  745.7 19.4 reduce-scatter.8
  767.5 21.6 reduce-scatter.4
where the time goes:
time: 811 us; the launch traced here: 804 us
  waiting for transfers between devices  521 us (64%)
  local copies, waits for them, and re-layouts  140 us (17%)
  matrix products  63.6 us (8%)
  other arithmetic  35.6 us (4%)
  starting transfers between devices  26.8 us (3%)
  between operations  17.2 us (2%)
    all_gather x1, waiting for transfers between devices, body(): block_weights = lax.all_gather(dense_weights, 'expert', axis=2, tiled=True)  430 us
    all_to_all x1, waiting for transfers between devices, body(): lax.all_to_all(outgoing, 'dp', split_axis=1, concat_axis=1, tiled=True)  59.6 us
    slice x1, local copies, waits for them, and re-layouts, body(): shared_gate_w = block_weights[0]  43 us
    dot_general x6, matrix products, contract_last(): lax.dot_general(left_side, right_side, (((1,), (1,)), ((), ())), preferre...  28.8 us
    all_to_all x1, waiting for transfers between devices, body(): lax.all_to_all(send_dy, 'expert', split_axis=0, concat_axis=0, tiled=True)  21.1 us
    gather x1, local copies, waits for them, and re-layouts, body(): outgoing = jnp.take(block_weights, my_units.reshape(-1), axis=1)  21 us
    unnamed x47, local copies, waits for them, and re-layouts  18.5 us
  transfers between devices with their start and end apart: 10, of which 5 were waited for; matrix products, arithmetic and copies ran while one was open for 26% of the time, Pallas kernels for 0%

commit v1 on v0

--- a/solution.py
+++ b/solution.py
@@ -33,7 +33,7 @@
     expert_count = lax.axis_size("expert")
     my_row = lax.axis_index("dp")
     my_col = lax.axis_index("expert")
-    block_weights = lax.all_gather(dense_weights, "expert", axis=2, tiled=True)
+    block_weights = jnp.concatenate(lax.all_gather(dense_weights, "expert"), axis=2)
     block_units = block_weights.shape[1]
     units_share = EH // dp_count
     pick_count = units_share // dp_count

time: 811 us -> 739 us (0.911)
  waiting for transfers between devices: 521 us -> 422 us
  local copies, waits for them, and re-layouts: 140 us -> 186 us
  matrix products: 63.6 us -> 44.3 us
    all_gather x1, waiting for transfers between devices: 430 us -> 320 us  [body(): lax.all_gather(dense_weights, 'expert')]
    reshape x0 -> x2, local copies, waits for them, and re-layouts: none -> 58.3 us  [body(): jnp.concatenate(lax.all_gather(dense_weights, 'expert'), axis=2)]
    slice x1 -> x2, local copies, waits for them, and re-layouts: 43 us -> 22 us  [body(): shared_gate_w = block_weights[0]]
    slice x1 -> x3, local copies, waits for them, and re-layouts: 0.21 us -> 17.2 us  [the longest x1 8.66 us: body(): shared_up_w = block_weights[1]]
    dot_general x6, matrix products: 28.8 us -> 14.4 us  [contract_last(): lax.dot_general(left_side, right_side, (((1,), (1,)), ((), ())), preferre...]
    reduce_scatter x1, waiting for transfers between devices: 0.02 us -> 10.1 us  [body(): lax.psum_scatter(shared_back.astype(jnp.bfloat16), 'dp', scatter_dimensio...]
    unnamed x47 -> x38, local copies, waits for them, and re-layouts: 18.5 us -> 9.8 us
  transfers between devices with their start and end apart: 10 -> 10, of which waited for: 5 -> 6; matrix products, arithmetic and copies ran while one was open for 26% -> 34% of each run, Pallas kernels for 0% -> 0%
where the time goes in v1:
time: 739 us; the launch traced here: 733 us
  waiting for transfers between devices  422 us (57%)
  local copies, waits for them, and re-layouts  186 us (25%)
  matrix products  44.3 us (6%)
  other arithmetic  36.3 us (5%)
  starting transfers between devices  26.9 us (4%)
  between operations  17.2 us (2%)
    all_gather x1, waiting for transfers between devices, body(): lax.all_gather(dense_weights, 'expert')  320 us
    all_to_all x1, waiting for transfers between devices, body(): lax.all_to_all(outgoing, 'dp', split_axis=1, concat_axis=1, tiled=True)  59.6 us
    reshape x2, local copies, waits for them, and re-layouts, body(): jnp.concatenate(lax.all_gather(dense_weights, 'expert'), axis=2)  58.3 us
    slice x2, local copies, waits for them, and re-layouts, body(): shared_gate_w = block_weights[0]  22 us
    all_to_all x1, waiting for transfers between devices, body(): lax.all_to_all(send_dy, 'expert', split_axis=0, concat_axis=0, tiled=True)  21.4 us
    gather x1, local copies, waits for them, and re-layouts, body(): outgoing = jnp.take(block_weights, my_units.reshape(-1), axis=1)  20.9 us
    gather x1, local copies, waits for them, and re-layouts, body(): expert_weights = jnp.take(arrived, jnp.argsort(my_order), axis=1)  16 us
  transfers between devices with their start and end apart: 10, of which 6 were waited for; matrix products, arithmetic and copies ran while one was open for 34% of the time, Pallas kernels for 0%

profile of v1, /device:TPU:0, one launch (start us, length us, event | category | flops | bytes accessed | tf_op | source)
XLA Modules:
  0.0 732.6 jit_solution(6725091540916594899)
XLA Ops:
  12.3 2.4 scatter_custom_fusion
  14.8 4.3 gather_fusion.4
  19.2 4.1 gather_fusion
  23.3 8.0 %all-to-all-start = ((bf16[8,80,2048]{2,1,0:T(8,128)(2,1)}), bf16[8,80,2048]{2,1,0:T(8,128)(2,1)S(1)}, u32[]{:S(2)}, u32[]{:S(2)}) async-start(bf16[8,80,2048]{2,1,0:T(8,128)(2,1)} %bitcast.86), calls=%async_computation.1 | async-start | bytes 5242880 | tf_op jit(solution)/shard_map/all_to_all | solution.py:80
  35.5 3.9 sort.34
  39.5 11.9 %gather_fusion.7 = s32[1408]{0:T(1024)S(1)} fusion(s32[4,352]{1,0:T(4,128)S(1)} %reshape.200, s32[1408]{0:T(1024)S(1)} %reshape.265), kind=kCustom, calls=%fused_computation.7 | custom fusion | bytes 22528 | tf_op jit(solution)/shard_map/jit(take_along_axis)/gather | solution.py:48
  52.9 320.3 %all-gather.3.cloned.1.call-done = bf16[24,1408,256]{2,1,0:T(8,128)(2,1)} async-done(((bf16[3,1408,256]{2,1,0:T(8,128)(2,1)}), bf16[24,1408,256]{2,1,0:T(8,128)(2,1)}) %all-gather.3.cloned.1.call-update) | async-done | bytes 17301520 | tf_op jit(solution)/shard_map/all_gather | solution.py:36
  373.3 20.9 %copy.35 = bf16[3,1408,8,256]{1,3,2,0:T(8,128)(2,1)} copy(bf16[3,1408,8,256]{3,1,0,2:T(8,128)(2,1)} %bitcast.78) | data formatting | bytes 34603008 | tf_op jit(solution)/shard_map/reshape | solution.py:36
  394.2 37.4 %copy.36 = bf16[3,1408,2048]{2,0,1:T(4,128)(2,1)} copy(bf16[3,1408,2048]{1,2,0:T(8,128)(2,1)} %bitcast.77) | data formatting | bytes 34603008 | tf_op jit(solution)/shard_map/reshape | solution.py:36
  431.6 20.9 %gather_fusion.1 = bf16[352,3,2048]{2,1,0:T(4,128)(2,1)} fusion(bf16[3,1408,2048]{2,0,1:T(4,128)(2,1)} %copy.36, s32[1024]{0:T(1024)S(1)} %pad_clamp_fusion.4), kind=kCustom, calls=%fused_computation.1 | custom fusion | bytes 8652160 | tf_op jit(solution)/shard_map/jit(_take)/gather | solution.py:52
  452.5 7.9 %select_bitcast_fusion.1 = bf16[3,352,2048]{2,0,1:T(4,128)(2,1)} fusion(bf16[352,3,2048]{2,1,0:T(4,128)(2,1)} %gather_fusion.1, pred[352]{0:T(512)(128)(4,1)S(1)} %compare_and_fusion), kind=kLoop, calls=%fused_computation.10 | loop fusion | flops 2162688 | bytes 8651104 | tf_op jit(solution)/shard_map/jit(_take)/select_n | solution.py:52
  461.9 5.1 all-to-all-start.1
  467.1 3.4 gather_fusion.5
  470.6 2.0 fusion
  472.5 59.6 %all-to-all-done.1 = bf16[3,352,2048]{2,0,1:T(4,128)(2,1)} async-done(((bf16[3,352,2048]{2,0,1:T(4,128)(2,1)}), bf16[3,352,2048]{2,0,1:T(4,128)(2,1)}, u32[]{:S(2)}, u32[]{:S(2)}) %all-to-all-start.1) | async-done | bytes 4325408 | tf_op jit(solution)/shard_map/all_to_all | solution.py:53
  532.1 4.6 all-to-all-start.3
  536.9 3.8 sort.35
  540.7 16.0 %gather_fusion.2 = bf16[352,3,2048]{2,1,0:T(4,128)(2,1)} fusion(bf16[3,352,2048]{2,0,1:T(4,128)(2,1)} %all-to-all-done.1, s32[1024]{0:T(1024)S(1)} %pad_clamp_fusion.3), kind=kCustom, calls=%fused_computation.2 | custom fusion | bytes 8652160 | tf_op jit(solution)/shard_map/jit(_take)/gather | solution.py:55
  556.8 5.4 select_bitcast_fusion
  562.2 6.4 fusion.36
  569.5 2.0 copy.52
  572.3 2.3 fusion.39
  574.5 21.4 %all-to-all-done.3 = bf16[8,80,2048]{2,1,0:T(8,128)(2,1)} async-done(((bf16[8,80,2048]{2,1,0:T(8,128)(2,1)}), bf16[8,80,2048]{2,1,0:T(8,128)(2,1)}, u32[]{:S(2)}, u32[]{:S(2)}) %all-to-all-start.3) | async-done | bytes 2621472 | tf_op jit(solution)/shard_map/all_to_all | solution.py:81
  596.0 3.7 fusion.8
  599.7 2.5 multiply_convert_fusion.1
  603.1 3.2 convolution_convert_fusion.1
  606.4 5.8 convolution_convert_fusion
  612.2 13.8 %fusion.35 = (bf16[1,1408,8,256]{3,1,0,2:T(8,128)(2,1)}, bf16[1,1408,8,256]{3,1,0,2:T(8,128)(2,1)}, bf16[1,1408,8,256]{3,1,0,2:T(8,128)(2,1)}) fusion(bf16[3,1408,8,256]{3,1,0,2:T(8,128)(2,1)} %bitcast.79), kind=kLoop, calls=%fused_computation.104 | loop fusion | bytes 34603008 | tf_op jit(solution)/shard_map/slice | solution.py:106
  626.0 8.2 %copy.28 = bf16[1,1408,8,256]{1,3,2,0:T(8,128)(2,1)} copy(bf16[1,1408,8,256]{3,1,0,2:T(8,128)(2,1)} %get-tuple-element.11) | data formatting | bytes 11534336 | tf_op jit(solution)/shard_map/slice | solution.py:106
  634.2 8.4 %copy.30 = bf16[1,1408,8,256]{1,3,2,0:T(8,128)(2,1)} copy(bf16[1,1408,8,256]{3,1,0,2:T(8,128)(2,1)} %get-tuple-element.12) | data formatting | bytes 11534336 | tf_op jit(solution)/shard_map/slice | solution.py:108
  642.6 8.7 %copy.29 = bf16[1,1408,8,256]{1,3,2,0:T(8,128)(2,1)} copy(bf16[1,1408,8,256]{3,1,0,2:T(8,128)(2,1)} %get-tuple-element.13) | data formatting | bytes 11534336 | tf_op jit(solution)/shard_map/slice | solution.py:107
  651.3 3.8 fusion.37
  656.6 1.6 copy-done.1
  659.3 2.8 convolution_convert_fusion.5
  662.1 4.3 all-to-all-start.2
  666.5 4.6 fusion.18
  671.1 5.5 fusion.7
  676.6 4.4 fusion.6
  681.0 3.1 all-to-all-done.2
  684.1 4.5 all-to-all-start.4
  688.7 2.4 fusion.4
  692.4 2.3 pad_maximum_fusion
  695.9 1.6 gather_fusion.3
  698.9 6.8 all-to-all-done.4
  706.9 1.6 gather_fusion.6
  709.9 1.9 reduce_sum.32
  712.5 1.6 add_convert_fusion.1
  714.1 10.1 %reduce-scatter.9.cloned.1.call-done = bf16[128,512]{1,0:T(8,128)(2,1)} async-done(((bf16[128,2048]{1,0:T(8,128)(2,1)}), bf16[128,512]{1,0:T(8,128)(2,1)}) %reduce-scatter.9.cloned.1.call-update) | async-done | bytes 131088 | tf_op jit(solution)/shard_map/reduce_scatter | solution.py:142
  (103 shorter events, 24.2 us)
Async XLA Ops:
  7.2 460.0 %copy-start = (bf16[128,2048]{1,0:T(8,128)(2,1)S(1)}, bf16[128,2048]{1,0:T(8,128)(2,1)}, u32[]{:S(2)}) copy-start(bf16[128,2048]{1,0:T(8,128)(2,1)} %param.9) | copy-start | bytes 1572868
  7.2 366.1 %all-gather.3.cloned.1.call-start = ((), (), s32[]{:S(2)}) async-start(), calls=%async_computation.13 | async-start | bytes 19464192 | tf_op jit(solution)/shard_map/all_gather | solution.py:36
  7.9 11.2 %copy-start.3 = (bf16[128,2048]{1,0:T(8,128)(2,1)S(1)}, bf16[128,2048]{1,0:T(8,128)(2,1)}, u32[]{:S(2)}) copy-start(bf16[128,2048]{1,0:T(8,128)(2,1)} %param.8) | copy-start | bytes 1572868
  23.3 8.0 %copy-start.13 = (s32[8]{0:T(128)S(1)}, s32[8]{0:T(128)}, u32[]{:S(2)}) copy-start(s32[8]{0:T(128)} %param.13) | copy-start | bytes 100
  23.3 437.1 %all-to-all-start = ((bf16[8,80,2048]{2,1,0:T(8,128)(2,1)}), bf16[8,80,2048]{2,1,0:T(8,128)(2,1)S(1)}, u32[]{:S(2)}, u32[]{:S(2)}) async-start(bf16[8,80,2048]{2,1,0:T(8,128)(2,1)} %bitcast.86), calls=%async_computation.1 | async-start | bytes 5242880 | tf_op jit(solution)/shard_map/all_to_all | solution.py:80
  460.4 1.5 copy-start.6
  461.9 70.2 %all-to-all-start.1 = ((bf16[3,352,2048]{2,0,1:T(4,128)(2,1)}), bf16[3,352,2048]{2,0,1:T(4,128)(2,1)}, u32[]{:S(2)}, u32[]{:S(2)}) async-start(bf16[3,352,2048]{2,0,1:T(4,128)(2,1)} %select_bitcast_fusion.1), calls=%async_computation.2 | async-start | bytes 11534336 | tf_op jit(solution)/shard_map/all_to_all | solution.py:53
  532.1 63.9 %all-to-all-start.3 = ((bf16[8,80,2048]{2,1,0:T(8,128)(2,1)}), bf16[8,80,2048]{2,1,0:T(8,128)(2,1)}, u32[]{:S(2)}, u32[]{:S(2)}) async-start(bf16[8,80,2048]{2,1,0:T(8,128)(2,1)} %fusion), calls=%async_computation.6 | async-start | bytes 5242880 | tf_op jit(solution)/shard_map/all_to_all | solution.py:81
  536.7 125.4 %reduce-scatter.7.cloned.1.call-start = ((), (), s32[]{:S(2)}) async-start(), calls=%async_computation.10 | async-start | bytes 3276800 | tf_op jit(solution)/shard_map/reduce_scatter | solution.py:121
  569.5 2.0 copy-start.10
  569.5 2.8 copy-start.7
  596.0 3.7 copy-start.8
  596.0 3.7 copy-start.11
  596.0 3.7 copy-start.16
  602.3 0.8 copy-start.14
  606.3 74.7 %reduce-scatter.11.cloned.1.call-start = ((), (), s32[]{:S(2)}) async-start(), calls=%async_computation.12 | async-start | bytes 3276800 | tf_op jit(solution)/shard_map/reduce_scatter | solution.py:124
  612.2 100.3 %reduce-scatter.5.cloned.1.call-start = ((), (), s32[]{:S(2)}) async-start(), calls=%async_computation.9 | async-start | bytes 655360 | tf_op jit(solution)/shard_map/reduce_scatter | solution.py:139
  642.6 8.7 %copy-start.4 = (bf16[128,2048]{1,0:T(8,128)(2,1)S(1)}, bf16[128,2048]{1,0:T(8,128)(2,1)}, u32[]{:S(2)}) copy-start(bf16[128,2048]{1,0:T(8,128)(2,1)} %param.8) | copy-start | bytes 1572868
  651.3 4.3 copy-start.2
  655.6 2.6 copy-start.1
  662.1 22.0 %all-to-all-start.2 = ((bf16[8,80,512]{2,1,0:T(8,128)(2,1)}), bf16[8,80,512]{2,1,0:T(8,128)(2,1)}, u32[]{:S(2)}, u32[]{:S(2)}) async-start(bf16[8,80,512]{2,1,0:T(8,128)(2,1)} %bitcast.97), calls=%async_computation.4 | async-start | bytes 1310720 | tf_op jit(solution)/shard_map/all_to_all | solution.py:129
  666.5 57.7 %reduce-scatter.9.cloned.1.call-start = ((), (), s32[]{:S(2)}) async-start(), calls=%async_computation.11 | async-start | bytes 655360 | tf_op jit(solution)/shard_map/reduce_scatter | solution.py:142
  676.6 12.0 %copy-start.9 = (bf16[8,80,2048]{2,1,0:T(8,128)(2,1)S(1)}, bf16[8,80,2048]{2,1,0:T(8,128)(2,1)}, u32[]{:S(2)}) copy-start(bf16[8,80,2048]{2,1,0:T(8,128)(2,1)} %copy-done.6) | copy-start | bytes 7864324
  684.1 21.5 %all-to-all-start.4 = ((bf16[8,80,512]{2,1,0:T(8,128)(2,1)}), bf16[8,80,512]{2,1,0:T(8,128)(2,1)}, u32[]{:S(2)}, u32[]{:S(2)}) async-start(bf16[8,80,512]{2,1,0:T(8,128)(2,1)} %bitcast.96), calls=%async_computation.8 | async-start | bytes 1310720 | tf_op jit(solution)/shard_map/all_to_all | solution.py:132
  688.6 2.4 copy-start.15
  691.0 1.4 copy-start.12
  708.5 3.2 copy-start.5
Sparse Core Ops, SparseCore 0:
  9.5 363.7 all-gather.2
  606.4 32.6 reduce-scatter.6
  641.7 34.3 reduce-scatter.10
  678.5 21.6 reduce-scatter.4
  702.5 21.6 reduce-scatter.8
